TPU v7x, 512 devices: a whole 4x4x16 slice. The times are simulated.
512 devices in a mesh: blk: 32 (over z, core), env: 16 (over y, x).
Axes of the slice: x: 4, y: 4, z: 16, core: 2. Of those that a mesh axis runs over, the one named last changes fastest.
Arguments:
- psi: float32 [4096, 1024], P('blk', 'env')
- env_left: bfloat16 [4096, 16, 1024], P('blk', 'env')
- env_right: bfloat16 [16, 1024, 1024], P('env')
- sector_tiles: int32 [16], replicated, may hold values from 1 to 8, as said below
- pairing: int32 [16, 16], replicated, may hold values from 0 to 15, as said below
- coupling: int32 [16, 16], replicated, may hold values from 0 to 1, as said below
Outputs:
- products: float32 [3, 4096, 1024], P(None, 'blk', 'env')
- quotients: float32 [3], replicated
- next_vector: float32 [4096, 1024], P('blk', 'env')
Inputs may be any that keep to these rules, and one draw needn't show every extreme that they name: Sector k covers tiles first_tile[k] to first_tile[k] + sector_tiles[k] - 1 of 128 rows; together the sectors cover all 32 tiles. Channel 0 maps every sector to itself: pairing[k, 0] = k. Channel 0 acts on every sector: coupling[k, 0] = 1.
All inputs are finite; a program needn't handle non-finite values.
Results may differ from a plain program's by a relative error of at most 0.0091.
Values may be sent and summed in bfloat16 or wider, within the bound.
No kernel may reach another device: no remote copies, remote signals or barrier semaphores. Data moves between devices by JAX's collectives and lax.ppermute only.
A program may use at most 64 MiB of HBM per device.

v0:
```python
import jax
import jax.numpy as jnp
from jax import lax
from jax.sharding import PartitionSpec as P

TILE = 128
ITERS = 3
EPSILON = 1e-06


def lookup_sources(sector_tiles, pairing, coupling, tile_ids, source_span):
    first_tile = jnp.cumsum(sector_tiles) - sector_tiles
    sector_ids = jnp.arange(sector_tiles.shape[0], dtype=jnp.int32)
    sector_of = jnp.sum((tile_ids[:, None] >= first_tile[None, :]).astype(jnp.int32), axis=1) - 1
    sector_pick = (sector_of[:, None] == sector_ids[None, :]).astype(jnp.int32)
    source_sector = jnp.sum(sector_pick[:, :, None] * pairing[None, :, :], axis=1)
    coupled = jnp.sum(sector_pick[:, :, None] * coupling[None, :, :], axis=1)
    source_pick = (source_sector[:, :, None] == sector_ids[None, None, :]).astype(jnp.int32)
    source_first = jnp.sum(source_pick * first_tile[None, None, :], axis=2) * TILE
    source_rows = jnp.sum(source_pick * sector_tiles[None, None, :], axis=2) * TILE
    offsets = jnp.arange(source_span, dtype=jnp.int32)
    keep_mask = (offsets[None, None, :] < source_rows[:, :, None]) & (coupled[:, :, None] == 1)
    return (source_first, keep_mask)


def per_device(psi, env_left, env_right, sector_tiles, pairing, coupling):
    row_count, col_width = psi.shape
    env_count = lax.axis_size("env")
    blk_count = lax.axis_size("blk")
    tile_local = row_count // TILE
    source_span = env_left.shape[2]
    local_terms = env_right.shape[0]
    all_terms = pairing.shape[1]
    full_width = col_width * env_count
    tile_ids = lax.axis_index("blk") * tile_local + jnp.arange(tile_local, dtype=jnp.int32)
    source_first, keep_mask = lookup_sources(sector_tiles, pairing, coupling, tile_ids, source_span)
    start_list = jnp.transpose(source_first).reshape(-1)
    term_first = lax.axis_index("env") * local_terms
    local_keep = lax.dynamic_slice_in_dim(keep_mask, term_first, local_terms, 1)
    left_panel = jnp.where(
        local_keep[:, None], env_left.reshape(tile_local, TILE, local_terms, source_span), 0
    )
    entry_count = float(row_count * blk_count * full_width)
    vector = psi
    product_list = []
    quotient_list = []
    for iteration in range(ITERS):
        rounded = vector.astype(jnp.bfloat16)
        every_row = lax.all_gather(rounded, "blk", axis=0, tiled=True)
        padded = jnp.concatenate(
            [every_row, jnp.zeros((source_span, col_width), jnp.bfloat16)], axis=0
        )
        source_slabs = jax.vmap(
            lambda first_row: lax.dynamic_slice_in_dim(padded, first_row, source_span, 0)
        )(start_list)
        source_slabs = source_slabs.reshape(all_terms, tile_local, source_span, col_width)
        moved_rows = lax.all_to_all(source_slabs, "env", split_axis=0, concat_axis=3, tiled=True)
        channel_mix = jnp.einsum(
            "dxtj,tdjc->tdxc", left_panel, moved_rows, preferred_element_type=jnp.float32
        )
        channel_mix = channel_mix.astype(jnp.bfloat16).reshape(local_terms, row_count, full_width)
        partial_sum = jnp.einsum(
            "trb,tbc->rc", channel_mix, env_right, preferred_element_type=jnp.float32
        )
        summed_all = lax.psum(partial_sum, "env")
        product = lax.dynamic_slice_in_dim(
            summed_all, lax.axis_index("env") * col_width, col_width, 1
        )
        inner_sum, square_sum = lax.psum(
            (jnp.sum(vector * product), jnp.sum(vector * vector)), ("blk", "env")
        )
        quotient = inner_sum / square_sum
        residual = product - quotient * vector
        energy = lax.psum(jnp.sum(residual * residual), ("blk", "env"))
        vector = residual * lax.rsqrt(energy / entry_count + EPSILON)
        product_list.append(product)
        quotient_list.append(quotient)
    return (jnp.stack(product_list), jnp.stack(quotient_list), vector)


def solution(mesh):
    placed = (P("blk", "env"), P("blk", "env", None), P("env", None, None), P(), P(), P())
    return jax.shard_map(
        per_device,
        mesh=mesh,
        in_specs=placed,
        out_specs=(P(None, "blk", "env"), P(), P("blk", "env")),
        check_vma=False,
    )
```

profile of v0, /device:TPU:1, one launch (start us, length us, event | category | flops | bytes accessed | tf_op | source)
XLA Modules:
  0.0 1310.4 jit_solution(9975891204792734560)
XLA Ops:
  12.6 39.0 %all_gather.9 = bf16[4096,64]{0,1:T(8,128)(2,1)S(1)} all-gather(bf16[128,64]{0,1:T(8,128)(2,1)S(1)} %convert_element_type.39), channel_id=1, replica_groups=mesh['blk'=32,'env'=16] {'blk'}, dimensions={0}, use_global_device_ids=true | all-gather | bytes 540672 | tf_op jit(solution)/shard_map/all_gather | solution.py:49
  51.6 1.6 broadcast.241.clone2
  53.2 37.1 %while.3 = (s32[]{:T(128)}, bf16[5120,64]{0,1:T(8,128)(2,1)S(1)}, s32[16,2]{0,1:T(2,128)S(1)}, bf16[16,1024,64]{1,2,0:T(8,128)(2,1)}, s32[]{:T(128)}) while((s32[]{:T(128)}, bf16[5120,64]{0,1:T(8,128)(2,1)S(1)}, s32[16,2]{0,1:T(2,128)S(1)}, bf16[16,1024,64]{1,2,0:T(8,128)(2,1)}, s32[]{:T(128)}) %tuple.64), condition=%wide.while_cond, body=%wide.while_body.sunk | while | flops 2 | bytes 1049181 | solution.py:54
  90.3 6.9 all-to-all-start
  99.8 30.3 %all-to-all-done = bf16[16,1,1024,64]{2,3,1,0:T(8,128)(2,1)} async-done(((bf16[16,1,1024,64]{2,3,1,0:T(8,128)(2,1)}), bf16[16,1,1024,64]{2,3,1,0:T(8,128)(2,1)}, u32[]{:S(2)}, u32[]{:S(2)}) %all-to-all-start) | async-done | bytes 2097184 | tf_op jit(solution)/shard_map/all_to_all | solution.py:57
  130.2 3.9 fusion.4
  134.1 107.7 %all-reduce.11.cloned.1.call-done = f32[128,1024]{0,1:T(8,128)} async-done(((f32[128,1024]{0,1:T(8,128)}), f32[128,1024]{0,1:T(8,128)}) %all-reduce.11.cloned.1.call-update) | async-done | bytes 524304 | tf_op jit(solution)/shard_map/psum | solution.py:65
  243.2 105.8 %all-reduce.6 = (f32[]{:T(128)}, f32[]{:T(128)}) all-reduce(f32[]{:T(128)} %get-tuple-element.76, f32[]{:T(128)} %get-tuple-element.75), channel_id=1, replica_groups=mesh['blk'=32,'env'=16] {'blk','env'}, use_global_device_ids=true, to_apply=%region_8.9 | all-reduce | flops 2 | bytes 16 | tf_op jit(solution)/shard_map/psum | solution.py:69
  351.7 99.5 %psum.87 = f32[]{:T(128)} all-reduce(f32[]{:T(128)} %get-tuple-element.113), channel_id=1, replica_groups=mesh['blk'=32,'env'=16] {'blk','env'}, use_global_device_ids=true, to_apply=%region_12.13 | all-reduce | flops 1 | bytes 8 | tf_op jit(solution)/shard_map/psum | solution.py:74
  451.9 29.6 %all_gather.10 = bf16[4096,64]{0,1:T(8,128)(2,1)S(1)} all-gather(bf16[128,64]{0,1:T(8,128)(2,1)S(1)} %multiply_convert_fusion.1), channel_id=1, replica_groups=mesh['blk'=32,'env'=16] {'blk'}, dimensions={0}, use_global_device_ids=true | all-gather | bytes 540672 | tf_op jit(solution)/shard_map/all_gather | solution.py:49
  481.6 1.6 broadcast.241.clone2.1
  483.2 37.2 %while.4 = (s32[]{:T(128)}, bf16[5120,64]{0,1:T(8,128)(2,1)S(1)}, s32[16,2]{0,1:T(2,128)S(1)}, bf16[16,1024,64]{1,2,0:T(8,128)(2,1)}, s32[]{:T(128)}) while((s32[]{:T(128)}, bf16[5120,64]{0,1:T(8,128)(2,1)S(1)}, s32[16,2]{0,1:T(2,128)S(1)}, bf16[16,1024,64]{1,2,0:T(8,128)(2,1)}, s32[]{:T(128)}) %tuple.79), condition=%wide.while_cond.1, body=%wide.while_body.1.sunk | while | flops 2 | bytes 1049181 | solution.py:54
  520.4 32.6 %all_to_all.45 = bf16[16,1,1024,64]{2,3,1,0:T(8,128)(2,1)} all-to-all(bf16[16,1,1024,64]{2,3,1,0:T(8,128)(2,1)} %bitcast.73), channel_id=1, replica_groups=mesh['blk'=32,'env'=16] {'env'}, dimensions={0} | all-to-all | bytes 4194304 | tf_op jit(solution)/shard_map/all_to_all | solution.py:57
  553.0 3.9 fusion.2
  557.0 108.5 %all-reduce.13.cloned.1.call-done = f32[128,1024]{0,1:T(8,128)} async-done(((f32[128,1024]{0,1:T(8,128)}), f32[128,1024]{0,1:T(8,128)}) %all-reduce.13.cloned.1.call-update) | async-done | bytes 524304 | tf_op jit(solution)/shard_map/psum | solution.py:65
  666.9 105.8 %all-reduce.5 = (f32[]{:T(128)}, f32[]{:T(128)}) all-reduce(f32[]{:T(128)} %get-tuple-element.74, f32[]{:T(128)} %get-tuple-element.73), channel_id=1, replica_groups=mesh['blk'=32,'env'=16] {'blk','env'}, use_global_device_ids=true, to_apply=%region_15.16 | all-reduce | flops 2 | bytes 16 | tf_op jit(solution)/shard_map/psum | solution.py:69
  775.4 99.5 %psum.91 = f32[]{:T(128)} all-reduce(f32[]{:T(128)} %get-tuple-element.111), channel_id=1, replica_groups=mesh['blk'=32,'env'=16] {'blk','env'}, use_global_device_ids=true, to_apply=%region_19.20 | all-reduce | flops 1 | bytes 8 | tf_op jit(solution)/shard_map/psum | solution.py:74
  875.7 29.6 %all_gather.11 = bf16[4096,64]{0,1:T(8,128)(2,1)S(1)} all-gather(bf16[128,64]{0,1:T(8,128)(2,1)S(1)} %multiply_convert_fusion), channel_id=1, replica_groups=mesh['blk'=32,'env'=16] {'blk'}, dimensions={0}, use_global_device_ids=true | all-gather | bytes 540672 | tf_op jit(solution)/shard_map/all_gather | solution.py:49
  907.0 39.1 %while.5 = (s32[]{:T(128)}, bf16[5120,64]{0,1:T(8,128)(2,1)S(1)}, s32[16,2]{0,1:T(2,128)S(1)}, bf16[16,1024,64]{1,2,0:T(8,128)(2,1)}, s32[]{:T(128)}) while((s32[]{:T(128)}, bf16[5120,64]{0,1:T(8,128)(2,1)S(1)}, s32[16,2]{0,1:T(2,128)S(1)}, bf16[16,1024,64]{1,2,0:T(8,128)(2,1)}, s32[]{:T(128)}) %tuple.80), condition=%wide.while_cond.2, body=%wide.while_body.2.sunk | while | flops 2 | bytes 1049181 | solution.py:54
  946.1 32.6 %all_to_all.46 = bf16[16,1,1024,64]{2,3,1,0:T(8,128)(2,1)} all-to-all(bf16[16,1,1024,64]{2,3,1,0:T(8,128)(2,1)} %bitcast.71), channel_id=1, replica_groups=mesh['blk'=32,'env'=16] {'env'}, dimensions={0} | all-to-all | bytes 4194304 | tf_op jit(solution)/shard_map/all_to_all | solution.py:57
  978.7 3.9 fusion
  982.6 108.6 %all-reduce.15.cloned.1.call-done = f32[128,1024]{0,1:T(8,128)} async-done(((f32[128,1024]{0,1:T(8,128)}), f32[128,1024]{0,1:T(8,128)}) %all-reduce.15.cloned.1.call-update) | async-done | bytes 524304 | tf_op jit(solution)/shard_map/psum | solution.py:65
  1092.5 105.8 %all-reduce.4 = (f32[]{:T(128)}, f32[]{:T(128)}) all-reduce(f32[]{:T(128)} %get-tuple-element.72, f32[]{:T(128)} %get-tuple-element.71), channel_id=1, replica_groups=mesh['blk'=32,'env'=16] {'blk','env'}, use_global_device_ids=true, to_apply=%region_22.23 | all-reduce | flops 2 | bytes 16 | tf_op jit(solution)/shard_map/psum | solution.py:69
  1201.1 99.5 %psum.95 = f32[]{:T(128)} all-reduce(f32[]{:T(128)} %multiply_reduce_fusion), channel_id=1, replica_groups=mesh['blk'=32,'env'=16] {'blk','env'}, use_global_device_ids=true, to_apply=%region_26.27 | all-reduce | flops 1 | bytes 8 | tf_op jit(solution)/shard_map/psum | solution.py:74
  (330 shorter events, 132.6 us)
Async XLA Ops:
  7.2 123.0 %copy-start = (bf16[1,1024,1024]{2,1,0:T(8,128)(2,1)S(1)}, bf16[1,1024,1024]{2,1,0:T(8,128)(2,1)}, u32[]{:S(2)}) copy-start(bf16[1,1024,1024]{2,1,0:T(8,128)(2,1)} %param.8) | copy-start | bytes 6291460
  90.3 39.8 %copy-start.1 = (bf16[128,1,1024]{2,0,1:T(8,128)(2,1)S(1)}, bf16[128,1,1024]{2,0,1:T(8,128)(2,1)}, u32[]{:S(2)}) copy-start(bf16[128,1,1024]{2,0,1:T(8,128)(2,1)} %param.7) | copy-start | bytes 786436
  90.3 39.8 %all-to-all-start = ((bf16[16,1,1024,64]{2,3,1,0:T(8,128)(2,1)}), bf16[16,1,1024,64]{2,3,1,0:T(8,128)(2,1)}, u32[]{:S(2)}, u32[]{:S(2)}) async-start(bf16[16,1,1024,64]{2,3,1,0:T(8,128)(2,1)} %bitcast.72), calls=%async_computation | async-start | bytes 4194304 | tf_op jit(solution)/shard_map/all_to_all | solution.py:57
  97.3 144.5 %all-reduce.11.cloned.1.call-start = ((), (), s32[]{:S(2)}) async-start(), calls=%async_computation.3 | async-start | bytes 1048576 | tf_op jit(solution)/shard_map/psum | solution.py:65
  130.2 111.6 %copy-start.2 = (f32[128,64]{0,1:T(8,128)S(1)}, f32[128,64]{0,1:T(8,128)}, u32[]{:S(2)}) copy-start(f32[128,64]{0,1:T(8,128)} %param.6) | copy-start | bytes 98308
  134.1 531.4 %all-reduce.13.cloned.1.call-start = ((), (), s32[]{:S(2)}) async-start(), calls=%async_computation.4 | async-start | bytes 1048576 | tf_op jit(solution)/shard_map/psum | solution.py:65
  556.9 534.2 %all-reduce.15.cloned.1.call-start = ((), (), s32[]{:S(2)}) async-start(), calls=%async_computation.5 | async-start | bytes 1048576 | tf_op jit(solution)/shard_map/psum | solution.py:65
Sparse Core Ops, SparseCore 0:
  134.2 107.5 all-reduce.10
  557.1 108.3 all-reduce.12
  982.7 108.4 all-reduce.14
where the time goes:
time: 1310 us
  blocking collectives  779 us (59%)
  waiting for transfers between devices  355 us (27%)
  local copies, waits for them, and re-layouts  119 us (9%)
  between operations  20.6 us (2%)
  other arithmetic  16.2 us (1%)
    psum x3, waiting for transfers between devices, per_device(): summed_all = lax.psum(partial_sum, 'env')  325 us
    psum x3, blocking collectives, per_device(): lax.psum((jnp.sum(vector * product), jnp.sum(vector * vector)), ('blk', '...  317 us
    psum x3, blocking collectives, per_device(): energy = lax.psum(jnp.sum(residual * residual), ('blk', 'env'))  299 us
    gather x288, local copies, waits for them, and re-layouts  112 us
    all_gather x3, blocking collectives, per_device(): every_row = lax.all_gather(rounded, 'blk', axis=0, tiled=True)  98.3 us
    all_to_all x2, blocking collectives, per_device(): lax.all_to_all(source_slabs, 'env', split_axis=0, concat_axis=3, tiled=True)  65.2 us
    all_to_all x1, waiting for transfers between devices, per_device(): lax.all_to_all(source_slabs, 'env', split_axis=0, concat_axis=3, tiled=True)  30.3 us
  transfers between devices with their start and end apart: 4, of which 4 were waited for; matrix products, arithmetic and copies ran while one was open for 0% of the time, Pallas kernels for 0%

commit v1 on v0

--- a/solution.py
+++ b/solution.py
@@ -1,3 +1,4 @@
+import functools
 import jax
 import jax.numpy as jnp
 from jax import lax
@@ -6,6 +7,14 @@
 TILE = 128
 ITERS = 3
 EPSILON = 1e-06
+
+
+def search_block_on_mesh(raw, which_axis):
+    near = jnp.sum(jax.lax.all_gather(raw, which_axis), 0)
+    return near
+
+
+time_the_clusters = functools.partial(search_block_on_mesh, which_axis="env")
 
 
 def lookup_sources(sector_tiles, pairing, coupling, tile_ids, source_span):
@@ -62,7 +71,7 @@
         partial_sum = jnp.einsum(
             "trb,tbc->rc", channel_mix, env_right, preferred_element_type=jnp.float32
         )
-        summed_all = lax.psum(partial_sum, "env")
+        summed_all = time_the_clusters(partial_sum)
         product = lax.dynamic_slice_in_dim(
             summed_all, lax.axis_index("env") * col_width, col_width, 1
         )

time: 1310 us -> 1260 us (0.962)
  waiting for transfers between devices: 355 us -> 269 us
  local copies, waits for them, and re-layouts: 119 us -> 147 us
    psum x3 -> x0, waiting for transfers between devices: 325 us -> none  [per_device(): summed_all = lax.psum(partial_sum, 'env')]
    all_gather x0 -> x3, waiting for transfers between devices: none -> 239 us  [search_block_on_mesh(): near = jnp.sum(jax.lax.all_gather(raw, which_axis), 0)]
    gather x288 -> x256, local copies, waits for them, and re-layouts: 112 us -> 136 us
    reduce_sum x0 -> x4, other arithmetic: none -> 13.4 us  [the longest x3 12.7 us: search_block_on_mesh(): near = jnp.sum(jax.lax.all_gather(raw, which_axis), 0)]
where the time goes in v1:
time: 1260 us
  blocking collectives  780 us (62%)
  waiting for transfers between devices  269 us (21%)
  local copies, waits for them, and re-layouts  147 us (12%)
  other arithmetic  23.7 us (2%)
  between operations  20.7 us (2%)
    psum x3, blocking collectives, per_device(): lax.psum((jnp.sum(vector * product), jnp.sum(vector * vector)), ('blk', '...  313 us
    psum x3, blocking collectives, per_device(): energy = lax.psum(jnp.sum(residual * residual), ('blk', 'env'))  301 us
    all_gather x3, waiting for transfers between devices, search_block_on_mesh(): near = jnp.sum(jax.lax.all_gather(raw, which_axis), 0)  239 us
    gather x256, local copies, waits for them, and re-layouts  136 us
    all_gather x3, blocking collectives, per_device(): every_row = lax.all_gather(rounded, 'blk', axis=0, tiled=True)  101 us
    all_to_all x2, blocking collectives, per_device(): lax.all_to_all(source_slabs, 'env', split_axis=0, concat_axis=3, tiled=True)  65.2 us
    all_to_all x1, waiting for transfers between devices, per_device(): lax.all_to_all(source_slabs, 'env', split_axis=0, concat_axis=3, tiled=True)  30.3 us
  transfers between devices with their start and end apart: 4, of which 4 were waited for; matrix products, arithmetic and copies ran while one was open for 0% of the time, Pallas kernels for 0%

profile of v1, /device:TPU:1, one launch (start us, length us, event | category | flops | bytes accessed | tf_op | source)
XLA Modules:
  0.0 1259.2 jit_solution(14174881208732632703)
XLA Ops:
  13.3 39.0 %all_gather.27 = bf16[4096,64]{0,1:T(8,128)(2,1)S(1)} all-gather(bf16[128,64]{0,1:T(8,128)(2,1)S(1)} %get-tuple-element.108), channel_id=1, replica_groups=mesh['blk'=32,'env'=16] {'blk'}, dimensions={0}, use_global_device_ids=true | all-gather | bytes 540672 | tf_op jit(solution)/shard_map/all_gather | solution.py:58
  53.9 39.1 %while.3 = (s32[]{:T(128)}, bf16[5120,64]{0,1:T(8,128)(2,1)S(1)}, s32[16,2]{0,1:T(2,128)S(1)}, bf16[16,1024,64]{1,2,0:T(8,128)(2,1)}, s32[]{:T(128)}) while((s32[]{:T(128)}, bf16[5120,64]{0,1:T(8,128)(2,1)S(1)}, s32[16,2]{0,1:T(2,128)S(1)}, bf16[16,1024,64]{1,2,0:T(8,128)(2,1)}, s32[]{:T(128)}) %tuple.62), condition=%wide.while_cond, body=%wide.while_body.sunk | while | flops 2 | bytes 1049181 | solution.py:63
  93.0 6.9 all-to-all-start
  102.5 30.3 %all-to-all-done = bf16[16,1,1024,64]{2,3,1,0:T(8,128)(2,1)} async-done(((bf16[16,1,1024,64]{2,3,1,0:T(8,128)(2,1)}), bf16[16,1,1024,64]{2,3,1,0:T(8,128)(2,1)}, u32[]{:S(2)}, u32[]{:S(2)}) %all-to-all-start) | async-done | bytes 2097184 | tf_op jit(solution)/shard_map/all_to_all | solution.py:66
  132.8 3.6 fusion.4
  136.6 79.2 %all-gather.7.cloned.1.call-done = f32[2048,1024]{1,0:T(8,128)} async-done(((f32[128,1024]{1,0:T(8,128)}), f32[2048,1024]{1,0:T(8,128)}) %all-gather.7.cloned.1.call-update) | async-done | bytes 8388624 | tf_op jit(solution)/shard_map/all_gather | solution.py:13
  215.7 4.2 reduce_sum.158
  220.7 104.2 %all-reduce.6 = (f32[]{:T(128)}, f32[]{:T(128)}) all-reduce(f32[]{:T(128)} %get-tuple-element.103, f32[]{:T(128)} %get-tuple-element.107), channel_id=1, replica_groups=mesh['blk'=32,'env'=16] {'blk','env'}, use_global_device_ids=true, to_apply=%region_8.9 | all-reduce | flops 2 | bytes 16 | tf_op jit(solution)/shard_map/psum | solution.py:78
  326.8 100.3 %psum.65 = f32[]{:T(128)} all-reduce(f32[]{:T(128)} %get-tuple-element.101), channel_id=1, replica_groups=mesh['blk'=32,'env'=16] {'blk','env'}, use_global_device_ids=true, to_apply=%region_12.13 | all-reduce | flops 1 | bytes 8 | tf_op jit(solution)/shard_map/psum | solution.py:83
  427.8 31.2 %all_gather.30 = bf16[4096,64]{1,0:T(8,128)(2,1)S(1)} all-gather(bf16[128,64]{1,0:T(8,128)(2,1)S(1)} %multiply_convert_fusion.1), channel_id=1, replica_groups=mesh['blk'=32,'env'=16] {'blk'}, dimensions={0}, use_global_device_ids=true | all-gather | bytes 540672 | tf_op jit(solution)/shard_map/all_gather | solution.py:58
  462.0 49.0 %while.4 = (s32[]{:T(128)}, bf16[5120,64]{1,0:T(8,128)(2,1)}, s32[16,2]{0,1:T(2,128)S(1)}, bf16[16,1024,64]{1,2,0:T(8,128)(2,1)}, s32[]{:T(128)}) while((s32[]{:T(128)}, bf16[5120,64]{1,0:T(8,128)(2,1)}, s32[16,2]{0,1:T(2,128)S(1)}, bf16[16,1024,64]{1,2,0:T(8,128)(2,1)}, s32[]{:T(128)}) %tuple.77), condition=%wide.while_cond.1, body=%wide.while_body.1.sunk | while | flops 2 | bytes 787037 | solution.py:63
  510.9 32.6 %all_to_all.45 = bf16[16,1,1024,64]{2,3,1,0:T(8,128)(2,1)} all-to-all(bf16[16,1,1024,64]{2,3,1,0:T(8,128)(2,1)} %bitcast.76), channel_id=1, replica_groups=mesh['blk'=32,'env'=16] {'env'}, dimensions={0} | all-to-all | bytes 4194304 | tf_op jit(solution)/shard_map/all_to_all | solution.py:66
  543.5 3.6 fusion.2
  547.2 80.0 %all-gather.9.cloned.1.call-done = f32[2048,1024]{1,0:T(8,128)} async-done(((f32[128,1024]{1,0:T(8,128)}), f32[2048,1024]{1,0:T(8,128)}) %all-gather.9.cloned.1.call-update) | async-done | bytes 8388624 | tf_op jit(solution)/shard_map/all_gather | solution.py:13
  627.2 4.2 reduce_sum.162
  632.1 104.2 %all-reduce.5 = (f32[]{:T(128)}, f32[]{:T(128)}) all-reduce(f32[]{:T(128)} %get-tuple-element.62, f32[]{:T(128)} %get-tuple-element.61), channel_id=1, replica_groups=mesh['blk'=32,'env'=16] {'blk','env'}, use_global_device_ids=true, to_apply=%region_15.16 | all-reduce | flops 2 | bytes 16 | tf_op jit(solution)/shard_map/psum | solution.py:78
  738.3 100.3 %psum.68 = f32[]{:T(128)} all-reduce(f32[]{:T(128)} %get-tuple-element.98), channel_id=1, replica_groups=mesh['blk'=32,'env'=16] {'blk','env'}, use_global_device_ids=true, to_apply=%region_19.20 | all-reduce | flops 1 | bytes 8 | tf_op jit(solution)/shard_map/psum | solution.py:83
  839.3 31.2 %all_gather.33 = bf16[4096,64]{1,0:T(8,128)(2,1)S(1)} all-gather(bf16[128,64]{1,0:T(8,128)(2,1)S(1)} %multiply_convert_fusion), channel_id=1, replica_groups=mesh['blk'=32,'env'=16] {'blk'}, dimensions={0}, use_global_device_ids=true | all-gather | bytes 540672 | tf_op jit(solution)/shard_map/all_gather | solution.py:58
  873.4 48.9 %while.5 = (s32[]{:T(128)}, bf16[5120,64]{1,0:T(8,128)(2,1)}, s32[16,2]{0,1:T(2,128)S(1)}, bf16[16,1024,64]{1,2,0:T(8,128)(2,1)}, s32[]{:T(128)}) while((s32[]{:T(128)}, bf16[5120,64]{1,0:T(8,128)(2,1)}, s32[16,2]{0,1:T(2,128)S(1)}, bf16[16,1024,64]{1,2,0:T(8,128)(2,1)}, s32[]{:T(128)}) %tuple.78), condition=%wide.while_cond.2, body=%wide.while_body.2.sunk | while | flops 2 | bytes 787037 | solution.py:63
  922.3 32.6 %all_to_all.46 = bf16[16,1,1024,64]{2,3,1,0:T(8,128)(2,1)} all-to-all(bf16[16,1,1024,64]{2,3,1,0:T(8,128)(2,1)} %bitcast.74), channel_id=1, replica_groups=mesh['blk'=32,'env'=16] {'env'}, dimensions={0} | all-to-all | bytes 4194304 | tf_op jit(solution)/shard_map/all_to_all | solution.py:66
  958.6 79.9 %all-gather.11.cloned.1.call-done = f32[2048,1024]{1,0:T(8,128)} async-done(((f32[128,1024]{1,0:T(8,128)}), f32[2048,1024]{1,0:T(8,128)}) %all-gather.11.cloned.1.call-update) | async-done | bytes 8388624 | tf_op jit(solution)/shard_map/all_gather | solution.py:13
  1038.6 4.2 reduce_sum.166
  1043.5 104.2 %all-reduce.4 = (f32[]{:T(128)}, f32[]{:T(128)}) all-reduce(f32[]{:T(128)} %get-tuple-element.60, f32[]{:T(128)} %get-tuple-element.59), channel_id=1, replica_groups=mesh['blk'=32,'env'=16] {'blk','env'}, use_global_device_ids=true, to_apply=%region_22.23 | all-reduce | flops 2 | bytes 16 | tf_op jit(solution)/shard_map/psum | solution.py:78
  1149.7 100.3 %psum.71 = f32[]{:T(128)} all-reduce(f32[]{:T(128)} %multiply_reduce_fusion), channel_id=1, replica_groups=mesh['blk'=32,'env'=16] {'blk','env'}, use_global_device_ids=true, to_apply=%region_26.27 | all-reduce | flops 1 | bytes 8 | tf_op jit(solution)/shard_map/psum | solution.py:83
  (306 shorter events, 161.5 us)
Async XLA Ops:
  7.2 125.7 %copy-start = (bf16[1,1024,1024]{2,1,0:T(8,128)(2,1)S(1)}, bf16[1,1024,1024]{2,1,0:T(8,128)(2,1)}, u32[]{:S(2)}) copy-start(bf16[1,1024,1024]{2,1,0:T(8,128)(2,1)} %param.8) | copy-start | bytes 6291460
  93.0 39.8 %copy-start.1 = (bf16[128,1,1024]{2,0,1:T(8,128)(2,1)S(1)}, bf16[128,1,1024]{2,0,1:T(8,128)(2,1)}, u32[]{:S(2)}) copy-start(bf16[128,1,1024]{2,0,1:T(8,128)(2,1)} %param.7) | copy-start | bytes 786436
  93.0 39.8 %all-to-all-start = ((bf16[16,1,1024,64]{2,3,1,0:T(8,128)(2,1)}), bf16[16,1,1024,64]{2,3,1,0:T(8,128)(2,1)}, u32[]{:S(2)}, u32[]{:S(2)}) async-start(bf16[16,1,1024,64]{2,3,1,0:T(8,128)(2,1)} %bitcast.75), calls=%async_computation | async-start | bytes 4194304 | tf_op jit(solution)/shard_map/all_to_all | solution.py:66
  99.9 115.8 %all-gather.7.cloned.1.call-start = ((), (), s32[]{:S(2)}) async-start(), calls=%async_computation.3 | async-start | bytes 8912896 | tf_op jit(solution)/shard_map/all_gather | solution.py:13
  132.8 3.6 copy-start.2
  136.4 490.8 %all-gather.9.cloned.1.call-start = ((), (), s32[]{:S(2)}) async-start(), calls=%async_computation.4 | async-start | bytes 8912896 | tf_op jit(solution)/shard_map/all_gather | solution.py:13
  547.1 491.4 %all-gather.11.cloned.1.call-start = ((), (), s32[]{:S(2)}) async-start(), calls=%async_computation.5 | async-start | bytes 8912896 | tf_op jit(solution)/shard_map/all_gather | solution.py:13
Sparse Core Ops, SparseCore 0:
  136.5 79.1 all-gather.6
  547.2 79.8 all-gather.8
  958.6 79.8 all-gather.10
